TPU v7x, 32 devices: a whole 2x2x4 slice. The times are simulated.
32 devices in a mesh: lat: 8 (over y, x, core), lon: 4 (over z).
Axes of the slice: x: 2, y: 2, z: 4, core: 2. Of those that a mesh axis runs over, the one named last changes fastest.
Arguments:
- adjoint: float32 [8, 8, 256, 512], P(None, None, 'lat', 'lon'), may hold values from -6 to 6
- transport: float32 [6, 8, 256, 512], P(None, None, 'lat', 'lon'), may hold values from 0.03 to 0.14
- cell_weight: float32 [256, 512], P('lat', 'lon'), may hold values from 0.1 to 1
- region_local: int32 [256, 512], P('lat', 'lon'), may hold values from 0 to 255
- tile_regions: int32 [32, 256], replicated, may hold values from 0 to 2047, as said below
- polar_rows: int32 [256], P('lat'), may hold values 0 or 1
- week_index: int32 [1], replicated, may hold values from 0 to 51
- grad_in: bfloat16 [2048, 416], P(('lat', 'lon')), may hold values from -6 to 6
- covariance: bfloat16 [2048, 2048], P(('lat', 'lon')), may hold values from -0.25 to 0.25
Outputs:
- adjoint_out: float32 [8, 8, 256, 512], P(None, None, 'lat', 'lon')
- precond: float32 [2048, 416], P(('lat', 'lon'))
Inputs may be any that keep to these rules, and one draw needn't show every extreme that they name: `tile_regions`: each row holds 256 different region numbers; with per = 8, entries o * per to o * per + per - 1 of a row lie in regions o * 64 to o * 64 + 63, for every o.
All inputs are finite; a program needn't handle non-finite values. No bound on the sum of `polar_rows` on one device may be relied on, other than what follows from the above.
Results may differ from a plain program's by a relative error of at most 0.00066.
Values may be sent and summed in bfloat16 or wider, within the bound.
No kernel may reach another device: no remote copies, remote signals or barrier semaphores. Data moves between devices by JAX's collectives and lax.ppermute only.
A program may use at most 128 MiB of HBM per device.

v0:
```python
import jax
import jax.numpy as jnp
from jax import lax
from jax.sharding import PartitionSpec as P


def extended(x, sides, width):
    for axis, dim in sides:
        size, length = (lax.axis_size(axis), x.shape[dim])
        up = [(i, (i + 1) % size) for i in range(size)]
        down = [(j, i) for i, j in up]
        last = lax.slice_in_dim(x, length - width, length, axis=dim)
        leading = lax.slice_in_dim(x, 0, width, axis=dim)
        before = lax.ppermute(last, axis, up)
        after = lax.ppermute(leading, axis, down)
        x = jnp.concatenate([before, x, after], axis=dim)
    return x


def advance(padded, rates):
    centre = padded[:, :, 1:-1, 1:-1]
    to_east = padded[:, :, 1:-1, 2:] - centre
    to_west = padded[:, :, 1:-1, :-2] - centre
    to_north = padded[:, :, 2:, 1:-1] - centre
    to_south = padded[:, :, :-2, 1:-1] - centre
    flat_zero = jnp.zeros_like(centre[:, :1])
    upper = jnp.concatenate([centre[:, 1:] - centre[:, :-1], flat_zero], axis=1)
    lower = jnp.concatenate([flat_zero, centre[:, :-1] - centre[:, 1:]], axis=1)
    return (
        centre
        + rates[0] * to_east
        + rates[1] * to_west
        + rates[2] * to_north
        + rates[3] * to_south
        + rates[4] * upper
        + rates[5] * lower
    )


def pole_mask(padded, margin, interior):
    band = lax.axis_index("lat")
    last_band = lax.axis_size("lat") - 1
    row_ids = jnp.arange(interior + 2 * margin, dtype=jnp.int32)
    outside = (row_ids < margin) & (band == 0) | (row_ids >= interior + margin) & (
        band == last_band
    )
    return jnp.where(outside[None, None, :, None], 0.0, padded)


def shards(
    adjoint,
    transport,
    cell_weight,
    region_local,
    tile_regions,
    polar_rows,
    week_index,
    grad_in,
    covariance,
):
    tracers, levels, lat_rows, lon_cols = adjoint.shape
    region_count = covariance.shape[1]
    own_rows = covariance.shape[0]
    week_cols = grad_in.shape[1] // tracers
    lon_count = lax.axis_size("lon")
    my_tile = lax.axis_index("lat") * lon_count + lax.axis_index("lon")
    base = jnp.dot(
        covariance,
        lax.all_gather(grad_in, ("lat", "lon"), axis=0, tiled=True),
        preferred_element_type=jnp.float32,
    )
    field = adjoint
    for repeat in range(2):
        padded = extended(field, (("lat", 2), ("lon", 3)), 1)
        field = advance(pole_mask(padded, 1, lat_rows), transport)
    row_sums = lax.psum(jnp.sum(field, axis=3), "lon")
    zonal = row_sums / (lon_cols * lon_count)
    flags = polar_rows.astype(jnp.float32)[None, None, :, None]
    adjoint_out = field + 0.5 * flags * (zonal[..., None] - field)
    surface = (adjoint_out[:, 0] * cell_weight[None]).reshape(tracers, -1)
    local_count = tile_regions.shape[1]
    one_hot = (
        region_local.reshape(1, -1) == jnp.arange(local_count, dtype=jnp.int32)[:, None]
    ).astype(jnp.float32)
    local_sums = lax.dot_general(
        one_hot,
        surface,
        (((1,), (1,)), ((), ())),
        precision=lax.Precision.HIGHEST,
        preferred_element_type=jnp.float32,
    )
    my_regions = lax.dynamic_index_in_dim(tile_regions, my_tile, 0, keepdims=False)
    dense = jnp.zeros((region_count, tracers), jnp.float32).at[my_regions].add(local_sums)
    fresh_all = lax.psum(dense, ("lat", "lon")).astype(jnp.bfloat16)
    added = jnp.dot(covariance, fresh_all, preferred_element_type=jnp.float32)
    week_hot = (jnp.arange(week_cols, dtype=jnp.int32) == week_index[0]).astype(jnp.float32)
    precond = (
        base.reshape(own_rows, week_cols, tracers) + week_hot[None, :, None] * added[:, None, :]
    )
    return (adjoint_out, precond.reshape(own_rows, week_cols * tracers))


def solution(mesh):
    in_specs = (
        P(None, None, "lat", "lon"),
        P(None, None, "lat", "lon"),
        P("lat", "lon"),
        P("lat", "lon"),
        P(),
        P("lat"),
        P(),
        P(("lat", "lon"), None),
        P(("lat", "lon"), None),
    )
    out_specs = (P(None, None, "lat", "lon"), P(("lat", "lon"), None))
    return jax.shard_map(shards, mesh=mesh, in_specs=in_specs, out_specs=out_specs, check_vma=False)
```

profile of v0, /device:TPU:0, one launch (start us, length us, event | category | flops | bytes accessed | tf_op | source)
XLA Modules:
  0.0 179.2 jit_solution(4061105329152444854)
XLA Ops:
  8.9 2.9 %collective-permute-start.1 = (f32[8,8,1,128]{3,1,2,0:T(8,128)S(1)}, f32[8,8,1,128]{3,1,2,0:T(8,128)S(1)}, u32[]{:S(2)}, u32[]{:S(2)}) collective-permute-start(f32[8,8,1,128]{3,1,2,0:T(8,128)S(1)} %bitcast.36), channel_id=1, source_target_pairs={{4,0},{8,4},{12,8},{16,12},{20,16},{24,20},{28,24},{0,28},{5,1},{9... | collective-permute-start | bytes 98312 | tf_op jit(solution)/shard_map/ppermute | solution.py:15
  13.8 3.6 %copy.81 = f32[8,8,32,128]{2,1,3,0:T(8,128)} copy(f32[8,8,32,128]{3,2,1,0:T(8,128)} %param.9) | data formatting | bytes 2097152 | tf_op args[0]
  17.4 2.6 %copy.80 = f32[8,8,1,128]{2,1,3,0:T(8,128)} copy(f32[8,8,1,128]{3,1,2,0:T(8,128)S(1)} %collective-permute-done) | data formatting | bytes 65536 | tf_op jit(solution)/shard_map/ppermute | solution.py:14
  20.1 2.6 %copy.82 = f32[8,8,1,128]{2,1,3,0:T(8,128)} copy(f32[8,8,1,128]{3,1,2,0:T(8,128)S(1)} %collective-permute-done.1) | data formatting | bytes 65536 | tf_op jit(solution)/shard_map/ppermute | solution.py:15
  23.6 2.3 %collective-permute-start.2 = (f32[8,8,34,1]{2,1,3,0:T(8,128)S(1)}, f32[8,8,34,1]{2,1,3,0:T(8,128)S(1)}, u32[]{:S(2)}, u32[]{:S(2)}) collective-permute-start(f32[8,8,34,1]{2,1,3,0:T(8,128)S(1)} %get-tuple-element.16), channel_id=1, source_target_pairs={{0,1},{1,2},{2,3},{3,0},{4,5},{5,6},{6,7},{7,4},{8,9},{9,10},{10,1... | collective-permute-start | bytes 26120 | tf_op jit(solution)/shard_map/ppermute | solution.py:14
  26.0 2.1 %collective-permute-start.3 = (f32[8,8,34,1]{2,1,3,0:T(8,128)S(1)}, f32[8,8,34,1]{2,1,3,0:T(8,128)S(1)}, u32[]{:S(2)}, u32[]{:S(2)}) collective-permute-start(f32[8,8,34,1]{2,1,3,0:T(8,128)S(1)} %get-tuple-element.17), channel_id=1, source_target_pairs={{1,0},{2,1},{3,2},{0,3},{5,4},{6,5},{7,6},{4,7},{9,8},{10,9},{11,1... | collective-permute-start | bytes 26120 | tf_op jit(solution)/shard_map/ppermute | solution.py:15
  33.4 5.8 %maximum_select_fusion = f32[8,8,34,130]{2,1,3,0:T(8,128)S(1)} fusion(f32[8,8,34,1]{2,1,3,0:T(8,128)S(1)} %collective-permute-done.3, f32[8,8,1,128]{2,1,3,0:T(8,128)} %copy.82, f32[8,8,32,128]{2,1,3,0:T(8,128)} %copy.81, f32[8,8,1,128]{2,1,3,0:T(8,128)} %copy.80, f32[8,8,34,1]{2,1,3,0:T(8,128)S(1)} %collective-permute-done.2, pred[34]{0:T(512)(128)(4,1)S(1)} %and_or_fusion), kind=kLoop, calls=%fused_computation.1 | loop fusion | flops 1414400 | bytes 2263074 | tf_op jit(solution)/shard_map/jit(_where)/select_n | solution.py:47
  39.2 2.2 %slice_subtract_fusion.11 = (f32[8,7,32,128]{2,1,3,0:T(8,128)S(1)}, f32[8,7,32,128]{2,1,3,0:T(8,128)S(1)}) fusion(f32[8,8,34,130]{2,1,3,0:T(8,128)S(1)} %maximum_select_fusion), kind=kLoop, calls=%fused_computation.37 | loop fusion | flops 458752 | bytes 3670016 | tf_op jit(solution)/shard_map/sub | solution.py:27
  41.4 6.1 %fusion.13 = f32[8,8,32,128]{2,1,3,0:T(8,128)S(1)} fusion(f32[8,8,34,130]{2,1,3,0:T(8,128)S(1)} %maximum_select_fusion, f32[8,7,32,128]{2,1,3,0:T(8,128)S(1)} %get-tuple-element.21, f32[8,7,32,128]{2,1,3,0:T(8,128)S(1)} %get-tuple-element.20, f32[8,32,128]{1,0,2:T(8,128)} %copy.88, f32[8,32,128]{1,0,2:T(8,128)} %copy.87, f32[8,32,128]{1,0,2:T(8,128)} %copy.86, ...), kind=kLoop, calls=%fused_computation.21 | loop fusion | flops 4194304 | bytes 8912896 | tf_op jit(solution)/shard_map/add | solution.py:30
  47.6 4.6 %fusion.29 = (f32[8,8,1,128]{2,1,3,0:T(8,128)}, f32[8,8,1,128]{2,1,3,0:T(8,128)}) fusion(f32[8,8,32,128]{2,1,3,0:T(8,128)S(1)} %fusion.13), kind=kLoop, calls=%fused_computation.66 | loop fusion | bytes 131072 | tf_op jit(solution)/shard_map/slice | solution.py:12
  52.2 2.8 %copy.89 = f32[8,8,1,128]{3,1,2,0:T(8,128)S(1)} copy(f32[8,8,1,128]{2,1,3,0:T(8,128)} %get-tuple-element.22) | data formatting | bytes 65536 | tf_op jit(solution)/shard_map/slice | solution.py:12
  55.1 2.9 %copy.90 = f32[8,8,1,128]{3,1,2,0:T(8,128)S(1)} copy(f32[8,8,1,128]{2,1,3,0:T(8,128)} %get-tuple-element.23) | data formatting | bytes 65536 | tf_op jit(solution)/shard_map/slice | solution.py:13
  58.0 2.9 %collective-permute-start.5 = (f32[8,8,1,128]{3,1,2,0:T(8,128)S(1)}, f32[8,8,1,128]{3,1,2,0:T(8,128)S(1)}, u32[]{:S(2)}, u32[]{:S(2)}) collective-permute-start(f32[8,8,1,128]{3,1,2,0:T(8,128)S(1)} %copy.90), channel_id=1, source_target_pairs={{4,0},{8,4},{12,8},{16,12},{20,16},{24,20},{28,24},{0,28},{5,1},{9... | collective-permute-start | bytes 98312 | tf_op jit(solution)/shard_map/ppermute | solution.py:15
  62.2 2.7 %copy.91 = f32[8,8,1,128]{2,1,3,0:T(8,128)} copy(f32[8,8,1,128]{3,1,2,0:T(8,128)S(1)} %collective-permute-done.4) | data formatting | bytes 65536 | tf_op jit(solution)/shard_map/ppermute | solution.py:14
  64.9 2.7 %copy.92 = f32[8,8,1,128]{2,1,3,0:T(8,128)} copy(f32[8,8,1,128]{3,1,2,0:T(8,128)S(1)} %collective-permute-done.5) | data formatting | bytes 65536 | tf_op jit(solution)/shard_map/ppermute | solution.py:15
  68.7 3.7 %collective-permute-start.7 = (f32[8,8,34,1]{2,1,3,0:T(8,128)S(1)}, f32[8,8,34,1]{2,1,3,0:T(8,128)S(1)}, u32[]{:S(2)}, u32[]{:S(2)}) collective-permute-start(f32[8,8,34,1]{2,1,3,0:T(8,128)S(1)} %get-tuple-element.15), channel_id=1, source_target_pairs={{1,0},{2,1},{3,2},{0,3},{5,4},{6,5},{7,6},{4,7},{9,8},{10,9},{11,1... | collective-permute-start | bytes 26120 | tf_op jit(solution)/shard_map/ppermute | solution.py:15
  74.3 5.8 %maximum_select_fusion.1 = f32[8,8,34,130]{2,1,3,0:T(8,128)S(1)} fusion(f32[8,8,34,1]{2,1,3,0:T(8,128)S(1)} %collective-permute-done.7, f32[8,8,1,128]{2,1,3,0:T(8,128)} %copy.92, f32[8,8,32,128]{2,1,3,0:T(8,128)} %copy-done.1, f32[8,8,1,128]{2,1,3,0:T(8,128)} %copy.91, f32[8,8,34,1]{2,1,3,0:T(8,128)S(1)} %collective-permute-done.6, ...), kind=kLoop, calls=%fused_computation.2 | loop fusion | flops 1414400 | bytes 2263074 | tf_op jit(solution)/shard_map/jit(_where)/select_n | solution.py:47
  80.2 2.2 %slice_subtract_fusion.9 = (f32[8,7,32,128]{2,1,3,0:T(8,128)S(1)}, f32[8,7,32,128]{2,1,3,0:T(8,128)S(1)}) fusion(f32[8,8,34,130]{2,1,3,0:T(8,128)S(1)} %maximum_select_fusion.1), kind=kLoop, calls=%fused_computation.35 | loop fusion | flops 458752 | bytes 3670016 | tf_op jit(solution)/shard_map/sub | solution.py:27
  82.5 6.0 %fusion.27 = (f32[8,8,32]{2,1,0:T(8,128)S(1)}, f32[8,8,32,128]{2,1,3,0:T(8,128)}) fusion(f32[8,7,32,128]{2,1,3,0:T(8,128)S(1)} %get-tuple-element.19, f32[8,32,128]{1,0,2:T(8,128)S(1)} %copy-done.7, f32[8,7,32,128]{2,1,3,0:T(8,128)S(1)} %get-tuple-element.18, f32[8,32,128]{1,0,2:T(8,128)S(1)} %copy-done.6, f32[8,8,34,130]{2,1,3,0:T(8,128)S(1)} %maximum_select_fusion.1, ...), kind=kLoop, calls=%fused_computation.65 | loop fusion | flops 4454400 | bytes 8921088 | tf_op jit(solution)/shard_map/reduce_sum | solution.py:76
  88.4 19.5 %psum.14 = f32[8,8,32]{2,1,0:T(8,128)S(1)} all-reduce(f32[8,8,32]{2,1,0:T(8,128)S(1)} %get-tuple-element.12), channel_id=1, replica_groups=mesh['lat'=8,'lon'=4] {'lon'}, use_global_device_ids=true, to_apply=%region_1.2 | all-reduce | flops 2048 | bytes 16384 | tf_op jit(solution)/shard_map/psum | solution.py:76
  108.0 2.6 %multiply_add_fusion = f32[8,8,32,128]{2,1,3,0:T(8,128)S(1)} fusion(f32[8,8,32,128]{2,1,3,0:T(8,128)} %get-tuple-element.13, f32[8,8,32]{2,1,0:T(8,128)S(1)} %broadcast_multiply_fusion, f32[32]{0:T(128)S(1)} %convert_multiply_fusion), kind=kLoop, calls=%fused_computation.32 | loop fusion | flops 786432 | bytes 2105472 | tf_op jit(solution)/shard_map/add | solution.py:79
  112.6 3.7 %copy.96 = f32[8,8,32,128]{3,2,1,0:T(8,128)} copy(f32[8,8,32,128]{2,1,3,0:T(8,128)} %copy-done.2) | data formatting | bytes 2097152
  120.1 49.0 %psum.15 = bf16[2048,8]{1,0:T(8,128)(2,1)S(1)} all-reduce(f32[2048,8]{1,0:T(8,128)S(1)} %scatter_custom_fusion), channel_id=1, replica_groups=mesh['lat'=8,'lon'=4] {'lat','lon'}, use_global_device_ids=true, to_apply=%region_3.4 | all-reduce | flops 16384 | bytes 98304 | tf_op jit(solution)/shard_map/psum | solution.py:94
  169.7 2.7 %convolution_add_fusion = f32[64,416]{1,0:T(8,128)} fusion(bf16[64,2048]{1,0:T(8,128)(2,1)S(1)} %copy-done, bf16[2048,416]{1,0:T(8,128)(2,1)} %all-gather.2.cloned.1.call-done, f32[64,416]{1,0:T(8,128)S(1)} %copy.95, f32[416]{0:T(512)S(1)} %mul.174), kind=kOutput, calls=%fused_computation.39 | convolution fusion | flops 109105152 | bytes 2180736 | tf_op jit(solution)/shard_map/dot_general | solution.py:67
  (59 shorter events, 20.0 us)
Async XLA Ops:
  7.2 162.0 %copy-start = (bf16[64,2048]{1,0:T(8,128)(2,1)S(1)}, bf16[64,2048]{1,0:T(8,128)(2,1)}, u32[]{:S(2)}) copy-start(bf16[64,2048]{1,0:T(8,128)(2,1)} %param.17) | copy-start | bytes 786436
  7.2 162.5 %all-gather.2.cloned.1.call-start = ((), (), s32[]{:S(2)}) async-start(), calls=%async_computation | async-start | bytes 2162688 | tf_op jit(solution)/shard_map/all_gather | solution.py:69
  8.3 9.1 %collective-permute-start = (f32[8,8,1,128]{3,1,2,0:T(8,128)S(1)}, f32[8,8,1,128]{3,1,2,0:T(8,128)S(1)}, u32[]{:S(2)}, u32[]{:S(2)}) collective-permute-start(f32[8,8,1,128]{3,1,2,0:T(8,128)S(1)} %bitcast.37), channel_id=1, source_target_pairs={{0,4},{4,8},{8,12},{12,16},{16,20},{20,24},{24,28},{28,0},{1,5},{5... | collective-permute-start | bytes 98312 | tf_op jit(solution)/shard_map/ppermute | solution.py:14
  8.9 11.2 %collective-permute-start.1 = (f32[8,8,1,128]{3,1,2,0:T(8,128)S(1)}, f32[8,8,1,128]{3,1,2,0:T(8,128)S(1)}, u32[]{:S(2)}, u32[]{:S(2)}) collective-permute-start(f32[8,8,1,128]{3,1,2,0:T(8,128)S(1)} %bitcast.36), channel_id=1, source_target_pairs={{4,0},{8,4},{12,8},{16,12},{20,16},{24,20},{28,24},{0,28},{5,1},{9... | collective-permute-start | bytes 98312 | tf_op jit(solution)/shard_map/ppermute | solution.py:15
  23.6 9.7 %collective-permute-start.2 = (f32[8,8,34,1]{2,1,3,0:T(8,128)S(1)}, f32[8,8,34,1]{2,1,3,0:T(8,128)S(1)}, u32[]{:S(2)}, u32[]{:S(2)}) collective-permute-start(f32[8,8,34,1]{2,1,3,0:T(8,128)S(1)} %get-tuple-element.16), channel_id=1, source_target_pairs={{0,1},{1,2},{2,3},{3,0},{4,5},{5,6},{6,7},{7,4},{8,9},{9,10},{10,1... | collective-permute-start | bytes 26120 | tf_op jit(solution)/shard_map/ppermute | solution.py:14
  26.0 7.4 %collective-permute-start.3 = (f32[8,8,34,1]{2,1,3,0:T(8,128)S(1)}, f32[8,8,34,1]{2,1,3,0:T(8,128)S(1)}, u32[]{:S(2)}, u32[]{:S(2)}) collective-permute-start(f32[8,8,34,1]{2,1,3,0:T(8,128)S(1)} %get-tuple-element.17), channel_id=1, source_target_pairs={{1,0},{2,1},{3,2},{0,3},{5,4},{6,5},{7,6},{4,7},{9,8},{10,9},{11,1... | collective-permute-start | bytes 26120 | tf_op jit(solution)/shard_map/ppermute | solution.py:15
  47.6 4.6 %copy-start.1 = (f32[8,8,32,128]{2,1,3,0:T(8,128)}, f32[8,8,32,128]{2,1,3,0:T(8,128)S(1)}, u32[]{:S(2)}) copy-start(f32[8,8,32,128]{2,1,3,0:T(8,128)S(1)} %fusion.13) | copy-start | bytes 3145732
  55.1 7.1 %collective-permute-start.4 = (f32[8,8,1,128]{3,1,2,0:T(8,128)S(1)}, f32[8,8,1,128]{3,1,2,0:T(8,128)S(1)}, u32[]{:S(2)}, u32[]{:S(2)}) collective-permute-start(f32[8,8,1,128]{3,1,2,0:T(8,128)S(1)} %copy.89), channel_id=1, source_target_pairs={{0,4},{4,8},{8,12},{12,16},{16,20},{20,24},{24,28},{28,0},{1,5},{5... | collective-permute-start | bytes 98312 | tf_op jit(solution)/shard_map/ppermute | solution.py:14
  58.0 6.9 %collective-permute-start.5 = (f32[8,8,1,128]{3,1,2,0:T(8,128)S(1)}, f32[8,8,1,128]{3,1,2,0:T(8,128)S(1)}, u32[]{:S(2)}, u32[]{:S(2)}) collective-permute-start(f32[8,8,1,128]{3,1,2,0:T(8,128)S(1)} %copy.90), channel_id=1, source_target_pairs={{4,0},{8,4},{12,8},{16,12},{20,16},{24,20},{28,24},{0,28},{5,1},{9... | collective-permute-start | bytes 98312 | tf_op jit(solution)/shard_map/ppermute | solution.py:15
  68.5 5.8 %collective-permute-start.6 = (f32[8,8,34,1]{2,1,3,0:T(8,128)S(1)}, f32[8,8,34,1]{2,1,3,0:T(8,128)S(1)}, u32[]{:S(2)}, u32[]{:S(2)}) collective-permute-start(f32[8,8,34,1]{2,1,3,0:T(8,128)S(1)} %get-tuple-element.14), channel_id=1, source_target_pairs={{0,1},{1,2},{2,3},{3,0},{4,5},{5,6},{6,7},{7,4},{8,9},{9,10},{10,1... | collective-permute-start | bytes 26120 | tf_op jit(solution)/shard_map/ppermute | solution.py:14
  68.7 5.6 %collective-permute-start.7 = (f32[8,8,34,1]{2,1,3,0:T(8,128)S(1)}, f32[8,8,34,1]{2,1,3,0:T(8,128)S(1)}, u32[]{:S(2)}, u32[]{:S(2)}) collective-permute-start(f32[8,8,34,1]{2,1,3,0:T(8,128)S(1)} %get-tuple-element.15), channel_id=1, source_target_pairs={{1,0},{2,1},{3,2},{0,3},{5,4},{6,5},{7,6},{4,7},{9,8},{10,9},{11,1... | collective-permute-start | bytes 26120 | tf_op jit(solution)/shard_map/ppermute | solution.py:15
  80.1 2.3 %copy-start.3 = (f32[8,32,128]{1,0,2:T(8,128)S(1)}, f32[8,32,128]{1,0,2:T(8,128)}, u32[]{:S(2)}) copy-start(f32[8,32,128]{1,0,2:T(8,128)} %copy.84) | copy-start | bytes 393220
  80.2 2.3 %copy-start.4 = (f32[8,32,128]{1,0,2:T(8,128)S(1)}, f32[8,32,128]{1,0,2:T(8,128)}, u32[]{:S(2)}) copy-start(f32[8,32,128]{1,0,2:T(8,128)} %copy.85) | copy-start | bytes 393220
  80.2 2.3 %copy-start.5 = (f32[8,32,128]{1,0,2:T(8,128)S(1)}, f32[8,32,128]{1,0,2:T(8,128)}, u32[]{:S(2)}) copy-start(f32[8,32,128]{1,0,2:T(8,128)} %copy.86) | copy-start | bytes 393220
  80.2 2.3 %copy-start.6 = (f32[8,32,128]{1,0,2:T(8,128)S(1)}, f32[8,32,128]{1,0,2:T(8,128)}, u32[]{:S(2)}) copy-start(f32[8,32,128]{1,0,2:T(8,128)} %copy.87) | copy-start | bytes 393220
  80.2 2.3 %copy-start.7 = (f32[8,32,128]{1,0,2:T(8,128)S(1)}, f32[8,32,128]{1,0,2:T(8,128)}, u32[]{:S(2)}) copy-start(f32[8,32,128]{1,0,2:T(8,128)} %copy.88) | copy-start | bytes 393220
  110.6 2.0 %copy-start.2 = (f32[8,8,32,128]{2,1,3,0:T(8,128)}, f32[8,8,32,128]{2,1,3,0:T(8,128)S(1)}, u32[]{:S(2)}) copy-start(f32[8,8,32,128]{2,1,3,0:T(8,128)S(1)} %multiply_add_fusion) | copy-start | bytes 3145732
  112.6 3.9 %copy-start.8 = (s32[32,128]{1,0:T(8,128)S(1)}, s32[32,128]{1,0:T(8,128)}, u32[]{:S(2)}) copy-start(s32[32,128]{1,0:T(8,128)} %param.12) | copy-start | bytes 49156
  112.6 3.9 %copy-start.9 = (f32[32,128]{1,0:T(8,128)S(1)}, f32[32,128]{1,0:T(8,128)}, u32[]{:S(2)}) copy-start(f32[32,128]{1,0:T(8,128)} %param.11) | copy-start | bytes 49156
  112.6 3.7 %slice-start = ((f32[8,8,32,128]{2,1,3,0:T(8,128)}), f32[8,1,32,128]{2,1,3,0:T(1,128)S(1)}, s32[]{:S(2)}) async-start(f32[8,8,32,128]{2,1,3,0:T(8,128)} %copy-done.2), calls=%async_computation.1 | async-start | bytes 1048576 | tf_op jit(solution)/shard_map/slice | solution.py:80
Sparse Core Ops, SparseCore 0:
  12.0 58.4 all-gather.1
where the time goes:
time: 180 us; the launch traced here: 179 us
  blocking collectives  68.5 us (38%)
  local copies, waits for them, and re-layouts  38.5 us (21%)
  other arithmetic  35.8 us (20%)
  between operations  15 us (8%)
  starting transfers between devices  14.7 us (8%)
  matrix products  4.95 us (3%)
    psum x1, blocking collectives, shards(): fresh_all = lax.psum(dense, ('lat', 'lon')).astype(jnp.bfloat16)  49 us
    psum x1, blocking collectives, shards(): row_sums = lax.psum(jnp.sum(field, axis=3), 'lon')  19.5 us
    select_n x2, other arithmetic, pole_mask(): return jnp.where(outside[None, None, :, None], 0.0, padded)  11.7 us
    ppermute x4, starting transfers between devices, extended(): after = lax.ppermute(leading, axis, down)  11.6 us
    unnamed x22, local copies, waits for them, and re-layouts  9.28 us
    slice x3, local copies, waits for them, and re-layouts, extended(): last = lax.slice_in_dim(x, length - width, length, axis=dim)  8.58 us
    add x1, other arithmetic, advance(): centre + rates[0] * to_east + rates[1] * to_west + rates[2] * to_north  6.13 us
    reduce_sum x1, other arithmetic, shards(): row_sums = lax.psum(jnp.sum(field, axis=3), 'lon')  5.98 us
  transfers between devices with their start and end apart: 9, of which 1 were waited for; matrix products, arithmetic and copies ran while one was open for 41% of the time, Pallas kernels for 0%

commit v1 on v0

--- a/solution.py
+++ b/solution.py
@@ -91,7 +91,7 @@
     )
     my_regions = lax.dynamic_index_in_dim(tile_regions, my_tile, 0, keepdims=False)
     dense = jnp.zeros((region_count, tracers), jnp.float32).at[my_regions].add(local_sums)
-    fresh_all = lax.psum(dense, ("lat", "lon")).astype(jnp.bfloat16)
+    fresh_all = jnp.sum(lax.all_gather(dense, ("lat", "lon")), axis=0).astype(jnp.bfloat16)
     added = jnp.dot(covariance, fresh_all, preferred_element_type=jnp.float32)
     week_hot = (jnp.arange(week_cols, dtype=jnp.int32) == week_index[0]).astype(jnp.float32)
     precond = (

time: 180 us -> 372 us (2.07)
  waiting for transfers between devices: 1.77 us -> 239 us
  blocking collectives: 68.5 us -> 15.8 us
  other arithmetic: 35.8 us -> 44.7 us
    all_gather x0 -> x1, waiting for transfers between devices: none -> 187 us  [shards(): lax.all_gather(dense, ('lat', 'lon'))]
    psum x1 -> x0, blocking collectives: 49 us -> none  [shards(): fresh_all = lax.psum(dense, ('lat', 'lon')).astype(jnp.bfloat16)]
    all_gather x1, waiting for transfers between devices: 0.02 us -> 44.9 us  [shards(): lax.all_gather(grad_in, ('lat', 'lon'), axis=0, tiled=True)]
    reduce_sum x0 -> x1, other arithmetic: none -> 12.2 us  [shards(): jnp.sum(lax.all_gather(dense, ('lat', 'lon')), axis=0).astype(jnp.bfloat16)]
    ppermute x4, waiting for transfers between devices: 1.72 us -> 5.99 us  [extended(): before = lax.ppermute(last, axis, up)]
    psum x1, blocking collectives: 19.5 us -> 15.8 us  [shards(): row_sums = lax.psum(jnp.sum(field, axis=3), 'lon')]
    unnamed x22 -> x30, local copies, waits for them, and re-layouts: 9.28 us -> 9.39 us
  transfers between devices with their start and end apart: 9 -> 10, of which waited for: 1 -> 6; matrix products, arithmetic and copies ran while one was open for 41% -> 10% of each run, Pallas kernels for 0% -> 0%
where the time goes in v1:
time: 372 us
  waiting for transfers between devices  239 us (64%)
  other arithmetic  44.7 us (12%)
  local copies, waits for them, and re-layouts  38.8 us (10%)
  blocking collectives  15.8 us (4%)
  between operations  15 us (4%)
  starting transfers between devices  13 us (3%)
  matrix products  4.95 us (1%)
    all_gather x1, waiting for transfers between devices, shards(): lax.all_gather(dense, ('lat', 'lon'))  187 us
    all_gather x1, waiting for transfers between devices, shards(): lax.all_gather(grad_in, ('lat', 'lon'), axis=0, tiled=True)  44.9 us
    psum x1, blocking collectives, shards(): row_sums = lax.psum(jnp.sum(field, axis=3), 'lon')  15.8 us
    ppermute x4, starting transfers between devices, extended(): after = lax.ppermute(leading, axis, down)  12.7 us
    reduce_sum x1, other arithmetic, shards(): jnp.sum(lax.all_gather(dense, ('lat', 'lon')), axis=0).astype(jnp.bfloat16)  12.2 us
    unnamed x30, local copies, waits for them, and re-layouts  9.39 us
    slice x3, local copies, waits for them, and re-layouts, extended(): last = lax.slice_in_dim(x, length - width, length, axis=dim)  8.57 us
    select_n x2, other arithmetic, pole_mask(): return jnp.where(outside[None, None, :, None], 0.0, padded)  8.17 us
  transfers between devices with their start and end apart: 10, of which 6 were waited for; matrix products, arithmetic and copies ran while one was open for 10% of the time, Pallas kernels for 0%

profile of v1, /device:TPU:0, one launch (start us, length us, event | category | flops | bytes accessed | tf_op | source)
XLA Modules:
  0.0 371.6 jit_solution(13629089094419648733)
XLA Ops:
  8.3 3.4 collective-permute-start.1
  13.0 3.7 copy.83
  16.7 2.6 copy.84
  19.3 2.7 copy.82
  22.9 3.7 collective-permute-start.3
  32.3 5.8 %maximum_select_fusion = f32[8,8,34,130]{2,1,3,0:T(8,128)S(1)} fusion(f32[8,8,34,1]{2,1,3,0:T(8,128)S(1)} %collective-permute-done.3, f32[8,8,1,128]{2,1,3,0:T(8,128)} %copy.84, f32[8,8,32,128]{2,1,3,0:T(8,128)} %copy.83, f32[8,8,1,128]{2,1,3,0:T(8,128)} %copy.82, f32[8,8,34,1]{2,1,3,0:T(8,128)S(1)} %collective-permute-done.2, pred[34]{0:T(512)(128)(4,1)S(1)} %and_or_fusion), kind=kLoop, calls=%fused_computation.1 | loop fusion | flops 1414400 | bytes 2263074 | tf_op jit(solution)/shard_map/jit(_where)/select_n | solution.py:47
  40.3 6.1 %fusion.13 = f32[8,8,32,128]{2,1,3,0:T(8,128)S(1)} fusion(f32[8,8,34,130]{2,1,3,0:T(8,128)S(1)} %maximum_select_fusion, f32[8,7,32,128]{2,1,3,0:T(8,128)S(1)} %get-tuple-element.21, f32[8,7,32,128]{2,1,3,0:T(8,128)S(1)} %get-tuple-element.20, f32[8,32,128]{1,0,2:T(8,128)S(1)} %copy.90, f32[8,32,128]{1,0,2:T(8,128)} %copy.89, f32[8,32,128]{1,0,2:T(8,128)} %copy.88, ...), kind=kLoop, calls=%fused_computation.21 | loop fusion | flops 4194304 | bytes 8912896 | tf_op jit(solution)/shard_map/add | solution.py:30
  46.5 4.6 %fusion.29 = (f32[8,8,1,128]{2,1,3,0:T(8,128)}, f32[8,8,1,128]{2,1,3,0:T(8,128)}) fusion(f32[8,8,32,128]{2,1,3,0:T(8,128)S(1)} %fusion.13), kind=kLoop, calls=%fused_computation.66 | loop fusion | bytes 131072 | tf_op jit(solution)/shard_map/slice | solution.py:12
  51.1 2.9 copy.92
  56.0 2.8 copy.91
  59.1 2.7 copy.94
  63.3 2.7 copy.93
  67.1 3.6 collective-permute-start.7
  72.3 4.1 %collective-permute-done.6 = f32[8,8,34,1]{2,1,3,0:T(8,128)S(1)} collective-permute-done((f32[8,8,34,1]{2,1,3,0:T(8,128)S(1)}, f32[8,8,34,1]{2,1,3,0:T(8,128)S(1)}, u32[]{:S(2)}, u32[]{:S(2)}) %collective-permute-start.6) | collective-permute-done | bytes 8736 | tf_op jit(solution)/shard_map/ppermute | solution.py:14
  76.4 2.3 maximum_select_fusion.1
  81.1 6.0 %fusion.27 = (f32[8,8,32]{2,1,0:T(8,128)S(1)}, f32[8,8,32,128]{2,1,3,0:T(8,128)}) fusion(f32[8,7,32,128]{2,1,3,0:T(8,128)S(1)} %get-tuple-element.19, f32[8,32,128]{1,0,2:T(8,128)S(1)} %copy.90, f32[8,7,32,128]{2,1,3,0:T(8,128)S(1)} %get-tuple-element.18, f32[8,32,128]{1,0,2:T(8,128)S(1)} %copy-done.6, f32[8,8,34,130]{2,1,3,0:T(8,128)S(1)} %maximum_select_fusion.1, ...), kind=kLoop, calls=%fused_computation.65 | loop fusion | flops 4454400 | bytes 8921088 | tf_op jit(solution)/shard_map/reduce_sum | solution.py:76
  87.1 15.8 %psum.7 = f32[8,8,32]{2,1,0:T(8,128)S(1)} all-reduce(f32[8,8,32]{2,1,0:T(8,128)S(1)} %get-tuple-element.12), channel_id=1, replica_groups=mesh['lat'=8,'lon'=4] {'lon'}, use_global_device_ids=true, to_apply=%region_1.2 | all-reduce | flops 2048 | bytes 16384 | tf_op jit(solution)/shard_map/psum | solution.py:76
  102.9 2.6 multiply_add_fusion
  110.1 2.4 scatter_custom_fusion
  114.1 3.6 copy.98
  117.7 186.8 %all-gather.6.cloned.1.call-done = f32[65536,8]{1,0:T(8,128)} async-done(((f32[2048,8]{1,0:T(8,128)}), f32[65536,8]{1,0:T(8,128)}) %all-gather.6.cloned.1.call-update) | async-done | bytes 2097168 | tf_op jit(solution)/shard_map/all_gather | solution.py:94
  304.5 12.2 %reduce_sum.19 = bf16[2048,8]{1,0:T(8,128)(2,1)S(1)} reduce(f32[32,2048,8]{2,1,0:T(8,128)} %bitcast.36, f32[]{:T(128)} %constant.8.clone.1), dimensions={0}, to_apply=%region_3.4 | reduce | flops 507904 | bytes 2129924 | tf_op jit(solution)/shard_map/reduce_sum | solution.py:94
  317.1 44.9 %all-gather.4.cloned.1.call-done = bf16[2048,416]{1,0:T(8,128)(2,1)} async-done(((bf16[64,416]{1,0:T(8,128)(2,1)}), bf16[2048,416]{1,0:T(8,128)(2,1)}) %all-gather.4.cloned.1.call-update) | async-done | bytes 1703952 | tf_op jit(solution)/shard_map/all_gather | solution.py:69
  362.0 2.7 convolution_add_fusion
  (69 shorter events, 25.9 us)
Async XLA Ops:
  7.2 309.5 %copy-start = (bf16[64,2048]{1,0:T(8,128)(2,1)S(1)}, bf16[64,2048]{1,0:T(8,128)(2,1)}, u32[]{:S(2)}) copy-start(bf16[64,2048]{1,0:T(8,128)(2,1)} %param.17) | copy-start | bytes 786436
  7.2 297.3 %all-gather.6.cloned.1.call-start = ((), (), s32[]{:S(2)}) async-start(), calls=%async_computation.1 | async-start | bytes 34603008 | tf_op jit(solution)/shard_map/all_gather | solution.py:94
  8.3 8.3 %collective-permute-start.1 = (f32[8,8,1,128]{3,1,2,0:T(8,128)S(1)}, f32[8,8,1,128]{3,1,2,0:T(8,128)S(1)}, u32[]{:S(2)}, u32[]{:S(2)}) collective-permute-start(f32[8,8,1,128]{3,1,2,0:T(8,128)S(1)} %bitcast.39), channel_id=1, source_target_pairs={{4,0},{8,4},{12,8},{16,12},{20,16},{24,20},{28,24},{0,28},{5,1},{9... | collective-permute-start | bytes 98312 | tf_op jit(solution)/shard_map/ppermute | solution.py:15
  11.8 7.5 %collective-permute-start = (f32[8,8,1,128]{3,1,2,0:T(8,128)S(1)}, f32[8,8,1,128]{3,1,2,0:T(8,128)S(1)}, u32[]{:S(2)}, u32[]{:S(2)}) collective-permute-start(f32[8,8,1,128]{3,1,2,0:T(8,128)S(1)} %bitcast.38), channel_id=1, source_target_pairs={{0,4},{4,8},{8,12},{12,16},{16,20},{20,24},{24,28},{28,0},{1,5},{5... | collective-permute-start | bytes 98312 | tf_op jit(solution)/shard_map/ppermute | solution.py:14
  22.9 9.0 %collective-permute-start.3 = (f32[8,8,34,1]{2,1,3,0:T(8,128)S(1)}, f32[8,8,34,1]{2,1,3,0:T(8,128)S(1)}, u32[]{:S(2)}, u32[]{:S(2)}) collective-permute-start(f32[8,8,34,1]{2,1,3,0:T(8,128)S(1)} %get-tuple-element.17), channel_id=1, source_target_pairs={{1,0},{2,1},{3,2},{0,3},{5,4},{6,5},{7,6},{4,7},{9,8},{10,9},{11,1... | collective-permute-start | bytes 26120 | tf_op jit(solution)/shard_map/ppermute | solution.py:15
  26.5 5.7 %collective-permute-start.2 = (f32[8,8,34,1]{2,1,3,0:T(8,128)S(1)}, f32[8,8,34,1]{2,1,3,0:T(8,128)S(1)}, u32[]{:S(2)}, u32[]{:S(2)}) collective-permute-start(f32[8,8,34,1]{2,1,3,0:T(8,128)S(1)} %get-tuple-element.16), channel_id=1, source_target_pairs={{0,1},{1,2},{2,3},{3,0},{4,5},{5,6},{6,7},{7,4},{8,9},{9,10},{10,1... | collective-permute-start | bytes 26120 | tf_op jit(solution)/shard_map/ppermute | solution.py:14
  46.5 4.6 %copy-start.1 = (f32[8,8,32,128]{2,1,3,0:T(8,128)}, f32[8,8,32,128]{2,1,3,0:T(8,128)S(1)}, u32[]{:S(2)}) copy-start(f32[8,8,32,128]{2,1,3,0:T(8,128)S(1)} %fusion.13) | copy-start | bytes 3145732
  51.1 8.0 %copy-start.13 = (s32[32]{0:T(128)S(1)}, s32[32]{0:T(128)}, u32[]{:S(2)}) copy-start(s32[32]{0:T(128)} %param.14) | copy-start | bytes 388
  54.0 5.2 %collective-permute-start.5 = (f32[8,8,1,128]{3,1,2,0:T(8,128)S(1)}, f32[8,8,1,128]{3,1,2,0:T(8,128)S(1)}, u32[]{:S(2)}, u32[]{:S(2)}) collective-permute-start(f32[8,8,1,128]{3,1,2,0:T(8,128)S(1)} %copy.92), channel_id=1, source_target_pairs={{4,0},{8,4},{12,8},{16,12},{20,16},{24,20},{28,24},{0,28},{5,1},{9... | collective-permute-start | bytes 98312 | tf_op jit(solution)/shard_map/ppermute | solution.py:15
  58.8 4.5 %collective-permute-start.4 = (f32[8,8,1,128]{3,1,2,0:T(8,128)S(1)}, f32[8,8,1,128]{3,1,2,0:T(8,128)S(1)}, u32[]{:S(2)}, u32[]{:S(2)}) collective-permute-start(f32[8,8,1,128]{3,1,2,0:T(8,128)S(1)} %copy.91), channel_id=1, source_target_pairs={{0,4},{4,8},{8,12},{12,16},{16,20},{20,24},{24,28},{28,0},{1,5},{5... | collective-permute-start | bytes 98312 | tf_op jit(solution)/shard_map/ppermute | solution.py:14
  66.0 10.4 %copy-start.2 = (f32[8,8,32,128]{2,1,3,0:T(8,128)S(1)}, f32[8,8,32,128]{2,1,3,0:T(8,128)}, u32[]{:S(2)}) copy-start(f32[8,8,32,128]{2,1,3,0:T(8,128)} %copy-done.1) | copy-start | bytes 3145732
  66.0 10.4 %copy-start.3 = (f32[8,8,1,128]{2,1,3,0:T(8,128)S(1)}, f32[8,8,1,128]{2,1,3,0:T(8,128)}, u32[]{:S(2)}) copy-start(f32[8,8,1,128]{2,1,3,0:T(8,128)} %copy.94) | copy-start | bytes 98308
  66.0 10.4 %copy-start.4 = (f32[8,8,1,128]{2,1,3,0:T(8,128)S(1)}, f32[8,8,1,128]{2,1,3,0:T(8,128)}, u32[]{:S(2)}) copy-start(f32[8,8,1,128]{2,1,3,0:T(8,128)} %copy.93) | copy-start | bytes 98308
  67.1 5.2 %collective-permute-start.7 = (f32[8,8,34,1]{2,1,3,0:T(8,128)S(1)}, f32[8,8,34,1]{2,1,3,0:T(8,128)S(1)}, u32[]{:S(2)}, u32[]{:S(2)}) collective-permute-start(f32[8,8,34,1]{2,1,3,0:T(8,128)S(1)} %get-tuple-element.15), channel_id=1, source_target_pairs={{1,0},{2,1},{3,2},{0,3},{5,4},{6,5},{7,6},{4,7},{9,8},{10,9},{11,1... | collective-permute-start | bytes 26120 | tf_op jit(solution)/shard_map/ppermute | solution.py:15
  70.7 5.7 %collective-permute-start.6 = (f32[8,8,34,1]{2,1,3,0:T(8,128)S(1)}, f32[8,8,34,1]{2,1,3,0:T(8,128)S(1)}, u32[]{:S(2)}, u32[]{:S(2)}) collective-permute-start(f32[8,8,34,1]{2,1,3,0:T(8,128)S(1)} %get-tuple-element.14), channel_id=1, source_target_pairs={{0,1},{1,2},{2,3},{3,0},{4,5},{5,6},{6,7},{7,4},{8,9},{9,10},{10,1... | collective-permute-start | bytes 26120 | tf_op jit(solution)/shard_map/ppermute | solution.py:14
  78.7 2.3 copy-start.6
  78.7 2.3 copy-start.7
  78.8 2.3 copy-start.8
  78.8 2.3 copy-start.9
  78.8 2.3 copy-start.10
  102.8 5.3 %copy-start.11 = (s32[32,128]{1,0:T(8,128)S(1)}, s32[32,128]{1,0:T(8,128)}, u32[]{:S(2)}) copy-start(s32[32,128]{1,0:T(8,128)} %param.12) | copy-start | bytes 49156
  102.8 5.3 %copy-start.12 = (f32[32,128]{1,0:T(8,128)S(1)}, f32[32,128]{1,0:T(8,128)}, u32[]{:S(2)}) copy-start(f32[32,128]{1,0:T(8,128)} %param.11) | copy-start | bytes 49156
  105.5 2.1 copy-start.5
  112.6 249.4 %all-gather.4.cloned.1.call-start = ((), (), s32[]{:S(2)}) async-start(), calls=%async_computation | async-start | bytes 2162688 | tf_op jit(solution)/shard_map/all_gather | solution.py:69
Sparse Core Ops, SparseCore 0:
  112.7 191.7 all-gather.5
  307.4 54.5 all-gather.3
